TPU v7x, 32 devices: a whole 2x2x4 slice. The times are simulated.
32 devices in a mesh: enc: 4 (over z), ctx: 8 (over y, x, core).
Axes of the slice: x: 2, y: 2, z: 4, core: 2. Of those that a mesh axis runs over, the one named last changes fastest.
Arguments:
- patches: bfloat16 [3072, 1280], P('enc'), may hold values from -17 to 17
- patch_image: int32 [3072], P('enc'), may hold values from 63 to 767, as said below
- vit_gain: float32 [1280], replicated, may hold values from 0.1 to 1.9
- vit_qkv: bfloat16 [1280, 16, 240], P(None, 'ctx')
- vit_proj: bfloat16 [1280, 1280], P('ctx'), may hold values from -0.15625 to 0.15625
- merge_gain: float32 [1280], replicated, may hold values from 0.1 to 1.9
- merge_up: bfloat16 [5120, 5120], P(None, 'ctx'), may hold values from -0.078125 to 0.078125
- merge_down: bfloat16 [5120, 8192], P('ctx', 'enc'), may hold values from -0.078125 to 0.078125
- text_embed: bfloat16 [3072, 8192], P('ctx', 'enc'), may hold values from -17 to 17
- placeholder_unit: int32 [3072], replicated, may hold values from -1 to 767, as said below
- doc_id: int32 [3072], replicated, may hold values from 0 to 15, never falling along the last dimension, each value on 1 to 1920 neighbouring positions
- dec_gain: float32 [8192], replicated, may hold values from 0.1 to 1.9
- dec_wq: bfloat16 [8192, 2048], P(None, 'enc')
- dec_wk: bfloat16 [8192, 512], P(None, 'enc')
- dec_wv: bfloat16 [8192, 512], P(None, 'enc'), may hold values from -0.0625 to 0.0625
Outputs:
- attended: bfloat16 [3072, 2048], P('ctx', 'enc')
Inputs may be any that keep to these rules, and one draw needn't show every extreme that they name: `patch_image`: the patches of an image are consecutive, start at a multiple of 4, number a multiple of 4 and at most 256, and lie within one aligned block of 768 patches; image numbers never fall and differ between images; in every such block some image has exactly 256 patches. `placeholder_unit`: -1 marks a text position. Every unit appears exactly once; the units of one image fill consecutive placeholders in their order; the placeholders of an aligned block of 384 positions are consecutive and number at most 192, and some block holds exactly 192. `doc_id`: document numbers never fall; a document has at most 1920 positions, and some document exactly 1920.
All inputs are finite; a program needn't handle non-finite values.
Results may differ from a plain program's by a relative error of at most 0.0085.
Values may be sent and summed in bfloat16 or wider, within the bound.
No kernel may reach another device: no remote copies, remote signals or barrier semaphores. Data moves between devices by JAX's collectives and lax.ppermute only.
A program may use at most 128 MiB of HBM per device.

v0:
```python
import math
import jax
import jax.numpy as jnp
from jax import lax
from jax.sharding import PartitionSpec as P

HD = 128
QPK = 4
EPSILON = 1e-06
NEGATIVE = -1e30


def layer_norm(values, scaling):
    widened = values.astype(jnp.float32)
    center = widened - jnp.mean(widened, axis=1, keepdims=True)
    spread = jnp.mean(center * center, axis=1, keepdims=True)
    return (center * lax.rsqrt(spread + EPSILON) * scaling).astype(jnp.bfloat16)


def image_attention(queries, keys_in, values_in, image_ids):
    head_count, row_count, head_width = queries.shape
    block_rows = math.gcd(row_count, 512)
    scaling = head_width ** (-0.5)

    def image_one_block(offset):
        query_block = lax.dynamic_slice_in_dim(queries, offset, block_rows, 1)
        block_ids = lax.dynamic_slice_in_dim(image_ids, offset, block_rows, 0)
        allowed = block_ids[:, None] == image_ids[None, :]
        scores = (
            jnp.einsum("hqd,hkd->hqk", query_block, keys_in, preferred_element_type=jnp.float32)
            * scaling
        )
        scores = jnp.where(allowed[None], scores, NEGATIVE)
        highest = jnp.max(scores, axis=2, keepdims=True)
        weights = jnp.exp(scores - highest)
        totals = jnp.sum(weights, axis=2, keepdims=True)
        mixture = jnp.einsum(
            "hqk,hkd->hqd",
            weights.astype(jnp.bfloat16),
            values_in,
            preferred_element_type=jnp.float32,
        )
        return (mixture / totals).astype(jnp.bfloat16)

    offsets = jnp.arange(row_count // block_rows, dtype=jnp.int32) * block_rows
    blocks = lax.map(image_one_block, offsets)
    return blocks.transpose(1, 0, 2, 3).reshape(head_count, row_count, head_width)


def body(
    patches,
    patch_image,
    vit_gain,
    vit_qkv,
    vit_proj,
    merge_gain,
    merge_up,
    merge_down,
    text_embed,
    placeholder_unit,
    doc_id,
    dec_gain,
    dec_wq,
    dec_wk,
    dec_wv,
):
    ctx_index = lax.axis_index("ctx")
    group_rows = patches.shape[0]
    head_count = vit_qkv.shape[1]
    head_width = vit_qkv.shape[2] // 3
    normed_patches = layer_norm(patches, vit_gain)
    packed = jnp.dot(
        normed_patches,
        vit_qkv.reshape(vit_qkv.shape[0], head_count * 3 * head_width),
        preferred_element_type=jnp.float32,
    )
    packed = (
        packed.astype(jnp.bfloat16)
        .reshape(group_rows, head_count, 3, head_width)
        .transpose(2, 1, 0, 3)
    )
    attended_patches = image_attention(packed[0], packed[1], packed[2], patch_image)
    flat_heads = attended_patches.transpose(1, 0, 2).reshape(group_rows, head_count * head_width)
    head_terms = jnp.dot(flat_heads, vit_proj, preferred_element_type=jnp.float32)
    summed = lax.psum(head_terms, "ctx")
    vit_out = (patches.astype(jnp.float32) + summed).astype(jnp.bfloat16)
    merge_input = layer_norm(lax.optimization_barrier(vit_out), merge_gain)
    unit_inputs = merge_input.reshape(group_rows // 4, 4 * merge_input.shape[1])
    hidden = jax.nn.gelu(
        jnp.dot(unit_inputs, merge_up, preferred_element_type=jnp.float32), approximate=False
    ).astype(jnp.bfloat16)
    all_hidden = lax.all_gather(hidden, "enc", axis=0, tiled=True)
    unit_total = all_hidden.shape[0]
    tok_rows = text_embed.shape[0]
    local_units = lax.dynamic_slice_in_dim(placeholder_unit, ctx_index * tok_rows, tok_rows, 0)
    present = local_units >= 0
    own_vision = lax.psum_scatter(
        jnp.dot(all_hidden, merge_down, preferred_element_type=jnp.float32),
        "ctx",
        scatter_dimension=0,
        tiled=True,
    ).astype(jnp.bfloat16)
    vision_all = lax.all_gather(own_vision, "ctx", axis=0, tiled=True)
    vision_local = jnp.take(vision_all, jnp.clip(local_units, 0, unit_total - 1), axis=0)
    sequence = jnp.where(present[:, None], vision_local, text_embed)
    full_rows = lax.all_gather(sequence, "enc", axis=1, tiled=True)
    widened = full_rows.astype(jnp.float32)
    row_scale = lax.rsqrt(jnp.mean(widened * widened, axis=1, keepdims=True) + EPSILON)
    normed = (widened * row_scale * dec_gain).astype(jnp.bfloat16)
    queries_flat = jnp.dot(normed, dec_wq, preferred_element_type=jnp.float32).astype(jnp.bfloat16)
    keys_local = jnp.dot(normed, dec_wk, preferred_element_type=jnp.float32).astype(jnp.bfloat16)
    values_local = jnp.dot(normed, dec_wv, preferred_element_type=jnp.float32).astype(jnp.bfloat16)
    kv_local = dec_wk.shape[1] // HD
    queries = queries_flat.reshape(tok_rows, kv_local, QPK, HD).transpose(1, 2, 0, 3)
    query_first = ctx_index * tok_rows
    query_pos = query_first + jnp.arange(tok_rows, dtype=jnp.int32)
    query_docs = lax.dynamic_slice_in_dim(doc_id, query_first, tok_rows, 0)
    scaling = HD ** (-0.5)
    start_state = (
        jnp.full((kv_local, QPK, tok_rows), NEGATIVE, jnp.float32),
        jnp.zeros((kv_local, QPK, tok_rows), jnp.float32),
        jnp.zeros((kv_local, QPK, tok_rows, HD), jnp.float32),
    )
    offset = jnp.int32(0)
    key_part = lax.all_gather(keys_local, "ctx", axis=0, tiled=True)
    value_part = lax.all_gather(values_local, "ctx", axis=0, tiled=True)
    key_count = key_part.shape[0]
    sub_rows = math.gcd(key_count, 512)
    last_doc = lax.dynamic_slice_in_dim(doc_id, offset + key_count - 1, 1, 0)[0]
    visible = (offset <= query_first + tok_rows - 1) & (last_doc >= query_docs[0])

    def update(current):

        def update_one_block(turn_index, inner_state):
            highest, totals, mixture = inner_state
            begin_row = turn_index * sub_rows
            keys_block = lax.dynamic_slice_in_dim(key_part, begin_row, sub_rows, 0).reshape(
                sub_rows, kv_local, HD
            )
            values_block = lax.dynamic_slice_in_dim(value_part, begin_row, sub_rows, 0).reshape(
                sub_rows, kv_local, HD
            )
            key_pos = begin_row + jnp.arange(sub_rows, dtype=jnp.int32)
            key_docs = lax.dynamic_slice_in_dim(doc_id, begin_row, sub_rows, 0)
            allowed = (key_pos[None, :] <= query_pos[:, None]) & (
                key_docs[None, :] == query_docs[:, None]
            )
            scores = (
                jnp.einsum(
                    "gjtd,sgd->gjts", queries, keys_block, preferred_element_type=jnp.float32
                )
                * scaling
            )
            new_peak = jnp.maximum(highest, jnp.max(jnp.where(allowed, scores, NEGATIVE), axis=3))
            factor = jnp.exp(highest - new_peak)
            weights = jnp.where(allowed, jnp.exp(scores - new_peak[..., None]), 0.0)
            totals = totals * factor + jnp.sum(weights, axis=3)
            mixture = mixture * factor[..., None] + jnp.einsum(
                "gjts,sgd->gjtd",
                weights.astype(jnp.bfloat16),
                values_block,
                preferred_element_type=jnp.float32,
            )
            return (new_peak, totals, mixture)

        return lax.fori_loop(0, key_count // sub_rows, update_one_block, current)

    def unchanged(current):
        return current

    finished = lax.cond(visible, update, unchanged, start_state)
    outputs = (finished[2] / finished[1][..., None]).astype(jnp.bfloat16)
    return outputs.transpose(2, 0, 1, 3).reshape(tok_rows, kv_local * QPK * HD)


def solution(mesh):
    placed = (
        P("enc", None),
        P("enc"),
        P(),
        P(None, "ctx", None),
        P("ctx", None),
        P(),
        P(None, "ctx"),
        P("ctx", "enc"),
        P("ctx", "enc"),
        P(),
        P(),
        P(),
        P(None, "enc"),
        P(None, "enc"),
        P(None, "enc"),
    )
    return jax.shard_map(
        body, mesh=mesh, in_specs=placed, out_specs=P("ctx", "enc"), check_vma=False
    )
```

profile of v0, /device:TPU:0, one launch (start us, length us, event | category | flops | bytes accessed | tf_op | source)
XLA Modules:
  0.0 467.7 jit_solution(1278942646428029388)
XLA Ops:
  6.6 2.0 convert_reduce_fusion
  9.5 1.3 fusion.56
  11.7 14.6 %while.28 = (s32[]{:T(128)}, bf16[3,2,256,80]{2,3,1,0:T(8,128)(2,1)}, s32[3]{0:T(128)S(1)}, s32[768]{0:T(1024)S(1)}, bf16[2,768,80]{1,2,0:T(8,128)(2,1)S(1)}, /*...) while((s32[]{:T(128)}, ...), condition=%wide.region_5.6_spmd, body=%wide.region_2.5_spmd.sunk | while | flops 128859136 | bytes 6767287 | solution.py:46
  15.3 1.2 fusion.105
  20.1 1.2 fusion.105
  25.0 1.2 fusion.105
  26.2 1.0 copy.26
  27.2 2.6 fusion.74
  29.9 80.8 %all-reduce.2.cloned.1.call-done = f32[768,1280]{1,0:T(8,128)} async-done(((f32[768,1280]{1,0:T(8,128)}), f32[768,1280]{1,0:T(8,128)}) %all-reduce.2.cloned.1.call-update) | async-done | bytes 3932176 | tf_op jit(solution)/shard_map/psum | solution.py:85
  110.6 3.1 fusion.50
  114.8 2.0 fusion.49
  116.8 4.1 reshape.149
  120.8 6.1 %fusion.61 = bf16[192,640]{1,0:T(8,128)(2,1)S(1)} fusion(bf16[192,5120]{1,0:T(8,128)(2,1)} %reshape.149, bf16[5120,640]{1,0:T(8,128)(2,1)} %param.27), kind=kOutput, calls=%fused_computation.81 | convolution fusion | flops 1266278400 | bytes 8765440 | tf_op jit(solution)/shard_map/dot_general | solution.py:90
  127.0 21.8 %all_gather.15 = bf16[768,640]{1,0:T(8,128)(2,1)S(1)} all-gather(bf16[192,640]{1,0:T(8,128)(2,1)S(1)} %fusion.61), channel_id=1, replica_groups=mesh['enc'=4,'ctx'=8] {'enc'}, dimensions={0}, use_global_device_ids=true | all-gather | bytes 1228800 | tf_op jit(solution)/shard_map/all_gather | solution.py:92
  148.8 4.5 fusion.75
  153.3 60.7 %reduce-scatter.2.cloned.1.call-done = f32[96,2048]{1,0:T(8,128)} async-done(((f32[768,2048]{1,0:T(8,128)}), f32[96,2048]{1,0:T(8,128)}) %reduce-scatter.2.cloned.1.call-update) | async-done | bytes 786448 | tf_op jit(solution)/shard_map/reduce_scatter | solution.py:97
  214.0 1.9 convert_element_type.68
  217.0 31.3 %all-gather.3.cloned.1.call-done = bf16[768,2048]{1,0:T(8,128)(2,1)} async-done(((bf16[96,2048]{1,0:T(8,128)(2,1)}), bf16[768,2048]{1,0:T(8,128)(2,1)}) %all-gather.3.cloned.1.call-update) | async-done | bytes 3145744 | tf_op jit(solution)/shard_map/all_gather | solution.py:103
  248.3 6.7 %gather_fusion = bf16[384,2048]{1,0:T(8,128)(2,1)S(1)} fusion(bf16[768,2048]{1,0:T(8,128)(2,1)} %all-gather.3.cloned.1.call-done, s32[1024]{0:T(1024)S(1)} %pad_clamp_fusion), kind=kCustom, calls=%fused_computation | custom fusion | bytes 3147264 | tf_op jit(solution)/shard_map/jit(_take)/gather | solution.py:104
  255.0 1.4 select_select_fusion
  257.2 1.3 dynamic_slice.40
  260.3 111.6 %all-gather.5.cloned.1.call-done = bf16[384,8192]{1,0:T(8,128)(2,1)} async-done(((bf16[384,2048]{1,0:T(8,128)(2,1)}), bf16[384,8192]{1,0:T(8,128)(2,1)}) %all-gather.5.cloned.1.call-update) | async-done | bytes 6291472 | tf_op jit(solution)/shard_map/all_gather | solution.py:106
  371.9 4.3 fusion.37
  376.5 3.7 convolution_convert_fusion.1
  380.2 11.4 %all_gather.19 = bf16[3072,128]{1,0:T(8,128)(2,1)} all-gather(bf16[384,128]{1,0:T(8,128)(2,1)S(1)} %convolution_convert_fusion.1), channel_id=1, replica_groups=mesh['enc'=4,'ctx'=8] {'ctx'}, dimensions={0}, use_global_device_ids=true | all-gather | bytes 884736 | tf_op jit(solution)/shard_map/all_gather | solution.py:126
  391.6 3.4 convolution_convert_fusion
  396.0 4.6 convolution_convert_fusion.2
  400.6 11.5 %all_gather.18 = bf16[3072,128]{1,0:T(8,128)(2,1)} all-gather(bf16[384,128]{1,0:T(8,128)(2,1)S(1)} %convolution_convert_fusion.2), channel_id=1, replica_groups=mesh['enc'=4,'ctx'=8] {'ctx'}, dimensions={0}, use_global_device_ids=true | all-gather | bytes 884736 | tf_op jit(solution)/shard_map/all_gather | solution.py:125
  412.2 46.3 %conditional.1 = (f32[1,4,384]{2,1,0:T(4,128)}, f32[1,4,384,128]{3,2,1,0:T(8,128)}) conditional(s32[]{:T(128)} %convert_element_type.60, () %tuple.31, (s32[]{:T(128)}, s32[384]{0:T(512)S(1)}, s32[3072]{0:T(1024)}, s32[384]{0:T(512)S(1)}, bf16[3072,128]{1,0:T(8,128)(2,1)}, /*index=5*/bf16[1,4,384,128]{3,2,1,0:T(8,128)(2,1)}, ...), branch_computations={%region_11.12_spmd, %region_12.17_spmd} | conditional | flops 412493696 | bytes 12566875 | solution.py:171
  412.2 46.3 %while.27 = (s32[]{:T(128)}, f32[1,4,384]{2,1,0:T(4,128)S(1)}, f32[1,4,384]{2,1,0:T(4,128)}, f32[1,4,384,128]{3,2,1,0:T(8,128)}, s32[384]{0:T(512)S(1)}, /*index...) while((s32[]{:T(128)}, f32[1,4,384]{2,1,0:T(4,128)S(1)}, ...), condition=%wide.region_16.16_spmd.clone, body=%wide.region_13.15_spmd.clone.sunk | while | flops 412493312 | bytes 12563663 | solution.py:166
  413.2 1.7 fusion.108
  414.9 2.8 fusion.111
  420.1 1.7 fusion.108
  421.8 3.1 fusion.111
  425.6 1.3 bitcast_add_fusion.2
  427.9 1.7 fusion.108
  429.7 3.1 fusion.111
  433.5 1.3 bitcast_add_fusion.2
  435.8 1.7 fusion.108
  437.6 3.1 fusion.111
  441.4 1.3 bitcast_add_fusion.2
  443.7 1.7 fusion.108
  445.5 3.1 fusion.111
  449.3 1.3 bitcast_add_fusion.2
  451.6 1.7 fusion.108
  453.4 3.1 fusion.111
  457.2 1.3 bitcast_add_fusion.2
  458.5 1.6 fusion.69
  (120 shorter events, 24.1 us)
Async XLA Ops:
  6.5 142.2 %copy-start = (bf16[640,2048]{1,0:T(8,128)(2,1)S(1)}, bf16[640,2048]{1,0:T(8,128)(2,1)}, u32[]{:S(2)}) copy-start(bf16[640,2048]{1,0:T(8,128)(2,1)} %param.28) | copy-start | bytes 7864324
  6.5 3.0 copy-start.12
  6.5 104.1 %all-reduce.2.cloned.1.call-start = ((), (), s32[]{:S(2)}) async-start(), calls=%async_computation.1 | async-start | bytes 7864320 | tf_op jit(solution)/shard_map/psum | solution.py:85
  6.5 2.3 copy-start.2
  6.6 3.0 copy-start.10
  9.5 2.1 copy-start.7
  11.7 15.5 %copy-start.5 = (bf16[160,1280]{1,0:T(8,128)(2,1)S(1)}, bf16[160,1280]{1,0:T(8,128)(2,1)}, u32[]{:S(2)}) copy-start(bf16[160,1280]{1,0:T(8,128)(2,1)} %param.25) | copy-start | bytes 1228804
  13.9 1.4 copy-start.6
  18.8 1.4 copy-start.6
  23.6 1.4 copy-start.6
  29.8 184.1 %reduce-scatter.2.cloned.1.call-start = ((), (), s32[]{:S(2)}) async-start(), calls=%async_computation.2 | async-start | bytes 7077888 | tf_op jit(solution)/shard_map/reduce_scatter | solution.py:97
  113.8 1.0 copy-start.8
  153.2 95.0 %all-gather.3.cloned.1.call-start = ((), (), s32[]{:S(2)}) async-start(), calls=%async_computation.3 | async-start | bytes 3538944 | tf_op jit(solution)/shard_map/all_gather | solution.py:103
  215.9 156.0 %all-gather.5.cloned.1.call-start = ((), (), s32[]{:S(2)}) async-start(), calls=%async_computation.4 | async-start | bytes 7864320 | tf_op jit(solution)/shard_map/all_gather | solution.py:106
  217.0 38.0 %copy-start.4 = (bf16[384,2048]{1,0:T(8,128)(2,1)S(1)}, bf16[384,2048]{1,0:T(8,128)(2,1)}, u32[]{:S(2)}) copy-start(bf16[384,2048]{1,0:T(8,128)(2,1)} %param.29) | copy-start | bytes 4718596
  256.4 119.8 %copy-start.11 = (f32[8192]{0:T(1024)S(1)}, f32[8192]{0:T(1024)}, u32[]{:S(2)}) copy-start(f32[8192]{0:T(1024)} %param.32) | copy-start | bytes 98308
  371.9 4.6 copy-start.3
  371.9 19.7 %slice-start = ((s8[8388608]{0:T(1024)(128)(4,1)}), s8[4194304]{0:T(1024)(128)(4,1)S(1)}, s32[]{:S(2)}) async-start(s8[8388608]{0:T(1024)(128)(4,1)} %bitcast.126), calls=%async_computation.5 | async-start | bytes 8388608
  376.5 15.1 %slice-start.1 = ((s8[8388608]{0:T(1024)(128)(4,1)}), s8[4194304]{0:T(1024)(128)(4,1)S(1)}, s32[]{:S(2)}) async-start(s8[8388608]{0:T(1024)(128)(4,1)} %bitcast.126), calls=%async_computation.6 | async-start | bytes 8388608
  391.6 4.4 copy-start.9
  458.5 2.7 copy-start.1
Sparse Core Ops, SparseCore 0:
  30.0 80.6 all-reduce.1
  153.4 60.5 reduce-scatter.1
  216.0 32.1 all-gather.2
  256.6 115.3 all-gather.4
where the time goes:
time: 469 us; the launch traced here: 468 us
  waiting for transfers between devices  284 us (61%)
  matrix products  60.8 us (13%)
  blocking collectives  44.7 us (10%)
  other arithmetic  33.3 us (7%)
  local copies, waits for them, and re-layouts  24.3 us (5%)
  between operations  14.6 us (3%)
  loops' own time  5.3 us (1%)
    all_gather x1, waiting for transfers between devices, body(): full_rows = lax.all_gather(sequence, 'enc', axis=1, tiled=True)  112 us
    psum x1, waiting for transfers between devices, body(): summed = lax.psum(head_terms, 'ctx')  80.8 us
    reduce_scatter x1, waiting for transfers between devices, body(): lax.psum_scatter(jnp.dot(all_hidden, merge_down, preferred_element_type=j...  60.7 us
    all_gather x1, waiting for transfers between devices, body(): vision_all = lax.all_gather(own_vision, 'ctx', axis=0, tiled=True)  31.3 us
    all_gather x1, blocking collectives, body(): all_hidden = lax.all_gather(hidden, 'enc', axis=0, tiled=True)  21.8 us
    dot_general x6, matrix products, update_one_block(): jnp.einsum('gjts,sgd->gjtd', weights.astype(jnp.bfloat16), values_block,...  18.4 us
    all_gather x1, blocking collectives, body(): key_part = lax.all_gather(keys_local, 'ctx', axis=0, tiled=True)  11.5 us
    all_gather x1, blocking collectives, body(): value_part = lax.all_gather(values_local, 'ctx', axis=0, tiled=True)  11.4 us
  transfers between devices with their start and end apart: 4, of which 4 were waited for; matrix products, arithmetic and copies ran while one was open for 1% of the time, Pallas kernels for 0%

commit v1 on v0

--- a/solution.py
+++ b/solution.py
@@ -1,3 +1,4 @@
+import functools
 import math
 import jax
 import jax.numpy as jnp
@@ -8,6 +9,13 @@
 QPK = 4
 EPSILON = 1e-06
 NEGATIVE = -1e30
+
+
+def regions_put(u, pos_dim):
+    return jnp.concatenate(lax.all_gather(u, "enc"), axis=pos_dim)
+
+
+view_the_patches = functools.partial(regions_put, pos_dim=1)
 
 
 def layer_norm(values, scaling):
@@ -103,7 +111,7 @@
     vision_all = lax.all_gather(own_vision, "ctx", axis=0, tiled=True)
     vision_local = jnp.take(vision_all, jnp.clip(local_units, 0, unit_total - 1), axis=0)
     sequence = jnp.where(present[:, None], vision_local, text_embed)
-    full_rows = lax.all_gather(sequence, "enc", axis=1, tiled=True)
+    full_rows = view_the_patches(sequence)
     widened = full_rows.astype(jnp.float32)
     row_scale = lax.rsqrt(jnp.mean(widened * widened, axis=1, keepdims=True) + EPSILON)
     normed = (widened * row_scale * dec_gain).astype(jnp.bfloat16)

time: 469 us -> 491 us (1.047)
  other arithmetic: 33.3 us -> 43.1 us
  local copies, waits for them, and re-layouts: 24.3 us -> 33.3 us
    convert_element_type x0 -> x1, other arithmetic: none -> 9.92 us  [body(): normed = (widened * row_scale * dec_gain).astype(jnp.bfloat16)]
    convert_element_type x0 -> x1, local copies, waits for them, and re-layouts: none -> 9.42 us  [body(): widened = full_rows.astype(jnp.float32)]
where the time goes in v1:
time: 491 us; the launch traced here: 490 us
  waiting for transfers between devices  284 us (58%)
  matrix products  64.2 us (13%)
  blocking collectives  44.7 us (9%)
  other arithmetic  43.1 us (9%)
  local copies, waits for them, and re-layouts  33.3 us (7%)
  between operations  14.6 us (3%)
  loops' own time  5.3 us (1%)
    all_gather x1, waiting for transfers between devices, regions_put(): return jnp.concatenate(lax.all_gather(u, 'enc'), axis=pos_dim)  112 us
    psum x1, waiting for transfers between devices, body(): summed = lax.psum(head_terms, 'ctx')  80.8 us
    reduce_scatter x1, waiting for transfers between devices, body(): lax.psum_scatter(jnp.dot(all_hidden, merge_down, preferred_element_type=j...  60.7 us
    all_gather x1, waiting for transfers between devices, body(): vision_all = lax.all_gather(own_vision, 'ctx', axis=0, tiled=True)  31.3 us
    all_gather x1, blocking collectives, body(): all_hidden = lax.all_gather(hidden, 'enc', axis=0, tiled=True)  21.8 us
    dot_general x6, matrix products, update_one_block(): jnp.einsum('gjts,sgd->gjtd', weights.astype(jnp.bfloat16), values_block,...  18.4 us
    all_gather x1, blocking collectives, body(): value_part = lax.all_gather(values_local, 'ctx', axis=0, tiled=True)  11.5 us
    all_gather x1, blocking collectives, body(): key_part = lax.all_gather(keys_local, 'ctx', axis=0, tiled=True)  11.4 us
  transfers between devices with their start and end apart: 4, of which 4 were waited for; matrix products, arithmetic and copies ran while one was open for 1% of the time, Pallas kernels for 0%

profile of v1, /device:TPU:0, one launch (start us, length us, event | category | flops | bytes accessed | tf_op | source)
XLA Modules:
  0.0 490.0 jit_solution(17910847157729960992)
XLA Ops:
  6.6 2.0 convert_reduce_fusion
  9.5 1.3 fusion.55
  11.7 14.6 %while.28 = (s32[]{:T(128)}, bf16[3,2,256,80]{2,3,1,0:T(8,128)(2,1)}, s32[3]{0:T(128)S(1)}, s32[768]{0:T(1024)S(1)}, bf16[2,768,80]{1,2,0:T(8,128)(2,1)S(1)}, /*...) while((s32[]{:T(128)}, ...), condition=%wide.region_5.6_spmd, body=%wide.region_2.5_spmd.sunk | while | flops 128859136 | bytes 6767287 | solution.py:54
  20.1 1.2 fusion.104
  25.0 1.2 fusion.104
  27.2 2.6 fusion.70
  29.9 80.8 %all-reduce.2.cloned.1.call-done = f32[768,1280]{1,0:T(8,128)} async-done(((f32[768,1280]{1,0:T(8,128)}), f32[768,1280]{1,0:T(8,128)}) %all-reduce.2.cloned.1.call-update) | async-done | bytes 3932176 | tf_op jit(solution)/shard_map/psum | solution.py:93
  110.6 3.1 fusion.49
  114.8 2.0 fusion.48
  116.8 4.1 reshape.153
  120.8 6.1 %fusion.60 = bf16[192,640]{1,0:T(8,128)(2,1)S(1)} fusion(bf16[192,5120]{1,0:T(8,128)(2,1)} %reshape.153, bf16[5120,640]{1,0:T(8,128)(2,1)} %param.27), kind=kOutput, calls=%fused_computation.80 | convolution fusion | flops 1266278400 | bytes 8765440 | tf_op jit(solution)/shard_map/dot_general | solution.py:98
  127.0 21.8 %all_gather.18 = bf16[768,640]{1,0:T(8,128)(2,1)S(1)} all-gather(bf16[192,640]{1,0:T(8,128)(2,1)S(1)} %fusion.60), channel_id=1, replica_groups=mesh['enc'=4,'ctx'=8] {'enc'}, dimensions={0}, use_global_device_ids=true | all-gather | bytes 1228800 | tf_op jit(solution)/shard_map/all_gather | solution.py:100
  148.8 4.5 fusion.71
  153.3 60.7 %reduce-scatter.2.cloned.1.call-done = f32[96,2048]{1,0:T(8,128)} async-done(((f32[768,2048]{1,0:T(8,128)}), f32[96,2048]{1,0:T(8,128)}) %reduce-scatter.2.cloned.1.call-update) | async-done | bytes 786448 | tf_op jit(solution)/shard_map/reduce_scatter | solution.py:105
  214.0 1.9 convert_element_type.78
  217.0 31.3 %all-gather.4.cloned.1.call-done = bf16[768,2048]{1,0:T(8,128)(2,1)} async-done(((bf16[96,2048]{1,0:T(8,128)(2,1)}), bf16[768,2048]{1,0:T(8,128)(2,1)}) %all-gather.4.cloned.1.call-update) | async-done | bytes 3145744 | tf_op jit(solution)/shard_map/all_gather | solution.py:111
  248.3 6.7 %gather_fusion = bf16[384,2048]{1,0:T(8,128)(2,1)S(1)} fusion(bf16[768,2048]{1,0:T(8,128)(2,1)} %all-gather.4.cloned.1.call-done, s32[1024]{0:T(1024)S(1)} %pad_clamp_fusion), kind=kCustom, calls=%fused_computation | custom fusion | bytes 3147264 | tf_op jit(solution)/shard_map/jit(_take)/gather | solution.py:112
  255.0 1.5 select_select_fusion
  257.2 1.3 dynamic_slice.40
  260.3 111.6 %all-gather.6.cloned.1.call-done = bf16[1536,2048]{1,0:T(8,128)(2,1)} async-done(((bf16[384,2048]{1,0:T(8,128)(2,1)}), bf16[1536,2048]{1,0:T(8,128)(2,1)}) %all-gather.6.cloned.1.call-update) | async-done | bytes 6291472 | tf_op jit(solution)/shard_map/all_gather | solution.py:15
  371.9 9.4 %copy.23 = f32[4,384,2048]{1,2,0:T(8,128)} copy(bf16[4,384,2048]{2,1,0:T(8,128)(2,1)} %bitcast.132) | data formatting | bytes 18874368 | tf_op jit(solution)/shard_map/convert_element_type | solution.py:115
  381.3 4.3 multiply_reduce_fusion
  385.6 9.9 %fusion.38 = bf16[384,8192]{0,1:T(8,128)(2,1)} fusion(f32[4,384,2048]{1,2,0:T(8,128)} %copy.23, f32[8192]{0:T(1024)S(1)} %copy-done.7, f32[384]{0:T(512)S(1)} %add_rsqrt_fusion.2), kind=kLoop, calls=%fused_computation.48 | loop fusion | flops 9437184 | bytes 18908672 | tf_op jit(solution)/shard_map/convert_element_type | solution.py:117
  395.6 5.7 %convolution_convert_fusion = bf16[384,512]{1,0:T(8,128)(2,1)S(1)} fusion(bf16[384,8192]{0,1:T(8,128)(2,1)} %fusion.38, bf16[8192,512]{1,0:T(8,128)(2,1)S(1)} %bitcast.135), kind=kOutput, calls=%fused_computation.72 | convolution fusion | flops 3221422080 | bytes 15073280 | tf_op jit(solution)/shard_map/dot_general | solution.py:118
  402.2 4.8 convolution_convert_fusion.2
  407.0 11.4 %all_gather.22 = bf16[3072,128]{1,0:T(8,128)(2,1)} all-gather(bf16[384,128]{1,0:T(8,128)(2,1)S(1)} %convolution_convert_fusion.2), channel_id=1, replica_groups=mesh['enc'=4,'ctx'=8] {'ctx'}, dimensions={0}, use_global_device_ids=true | all-gather | bytes 884736 | tf_op jit(solution)/shard_map/all_gather | solution.py:133
  418.4 4.7 convolution_convert_fusion.1
  423.1 11.5 %all_gather.23 = bf16[3072,128]{1,0:T(8,128)(2,1)} all-gather(bf16[384,128]{1,0:T(8,128)(2,1)S(1)} %convolution_convert_fusion.1), channel_id=1, replica_groups=mesh['enc'=4,'ctx'=8] {'ctx'}, dimensions={0}, use_global_device_ids=true | all-gather | bytes 884736 | tf_op jit(solution)/shard_map/all_gather | solution.py:134
  434.5 46.2 %conditional.1 = (f32[1,4,384]{2,1,0:T(4,128)}, f32[1,4,384,128]{3,2,1,0:T(8,128)}) conditional(s32[]{:T(128)} %convert_element_type.70, () %tuple.31, (s32[]{:T(128)}, s32[384]{0:T(512)S(1)}, s32[3072]{0:T(1024)}, s32[384]{0:T(512)S(1)}, bf16[3072,128]{1,0:T(8,128)(2,1)}, /*index=5*/bf16[1,4,384,128]{3,2,1,0:T(8,128)(2,1)}, ...), branch_computations={%region_11.12_spmd, %region_12.17_spmd} | conditional | flops 412493696 | bytes 12566875 | solution.py:179
  434.6 46.2 %while.27 = (s32[]{:T(128)}, f32[1,4,384]{2,1,0:T(4,128)S(1)}, f32[1,4,384]{2,1,0:T(4,128)}, f32[1,4,384,128]{3,2,1,0:T(8,128)}, s32[384]{0:T(512)S(1)}, /*index...) while((s32[]{:T(128)}, f32[1,4,384]{2,1,0:T(4,128)S(1)}, ...), condition=%wide.region_16.16_spmd.clone, body=%wide.region_13.15_spmd.clone.sunk | while | flops 412493312 | bytes 12563663 | solution.py:174
  435.6 1.7 fusion.107
  437.3 2.8 fusion.110
  442.4 1.7 fusion.107
  444.2 3.1 fusion.110
  448.0 1.3 bitcast_add_fusion.2
  450.3 1.7 fusion.107
  452.1 3.1 fusion.110
  455.9 1.3 bitcast_add_fusion.2
  458.2 1.7 fusion.107
  460.0 3.1 fusion.110
  463.7 1.3 bitcast_add_fusion.2
  466.0 1.7 fusion.107
  467.8 3.1 fusion.110
  471.6 1.3 bitcast_add_fusion.2
  473.9 1.7 fusion.107
  475.7 3.1 fusion.110
  479.5 1.3 bitcast_add_fusion.2
  480.8 1.6 fusion.68
  (122 shorter events, 25.9 us)
Async XLA Ops:
  6.5 142.2 %copy-start = (bf16[640,2048]{1,0:T(8,128)(2,1)S(1)}, bf16[640,2048]{1,0:T(8,128)(2,1)}, u32[]{:S(2)}) copy-start(bf16[640,2048]{1,0:T(8,128)(2,1)} %param.28) | copy-start | bytes 7864324
  6.5 3.0 copy-start.12
  6.5 104.1 %all-reduce.2.cloned.1.call-start = ((), (), s32[]{:S(2)}) async-start(), calls=%async_computation.1 | async-start | bytes 7864320 | tf_op jit(solution)/shard_map/psum | solution.py:93
  6.5 2.3 copy-start.2
  6.6 3.0 copy-start.11
  9.5 2.1 copy-start.6
  11.7 15.5 %copy-start.4 = (bf16[160,1280]{1,0:T(8,128)(2,1)S(1)}, bf16[160,1280]{1,0:T(8,128)(2,1)}, u32[]{:S(2)}) copy-start(bf16[160,1280]{1,0:T(8,128)(2,1)} %param.25) | copy-start | bytes 1228804
  13.9 1.4 copy-start.5
  18.8 1.4 copy-start.5
  23.6 1.4 copy-start.5
  29.8 184.1 %reduce-scatter.2.cloned.1.call-start = ((), (), s32[]{:S(2)}) async-start(), calls=%async_computation.2 | async-start | bytes 7077888 | tf_op jit(solution)/shard_map/reduce_scatter | solution.py:105
  113.8 1.0 copy-start.8
  153.2 95.0 %all-gather.4.cloned.1.call-start = ((), (), s32[]{:S(2)}) async-start(), calls=%async_computation.3 | async-start | bytes 3538944 | tf_op jit(solution)/shard_map/all_gather | solution.py:111
  215.9 156.0 %all-gather.6.cloned.1.call-start = ((), (), s32[]{:S(2)}) async-start(), calls=%async_computation.4 | async-start | bytes 7864320 | tf_op jit(solution)/shard_map/all_gather | solution.py:15
  217.0 38.0 %copy-start.3 = (bf16[384,2048]{1,0:T(8,128)(2,1)S(1)}, bf16[384,2048]{1,0:T(8,128)(2,1)}, u32[]{:S(2)}) copy-start(bf16[384,2048]{1,0:T(8,128)(2,1)} %param.29) | copy-start | bytes 4718596
  381.3 4.3 copy-start.7
  381.3 14.2 %slice-start = ((s8[8388608]{0:T(1024)(128)(4,1)}), s8[4194304]{0:T(1024)(128)(4,1)S(1)}, s32[]{:S(2)}) async-start(s8[8388608]{0:T(1024)(128)(4,1)} %bitcast.134), calls=%async_computation.5 | async-start | bytes 8388608
  385.6 9.9 %slice-start.1 = ((s8[8388608]{0:T(1024)(128)(4,1)}), s8[4194304]{0:T(1024)(128)(4,1)S(1)}, s32[]{:S(2)}) async-start(s8[8388608]{0:T(1024)(128)(4,1)} %bitcast.134), calls=%async_computation.6 | async-start | bytes 8388608
  395.6 6.6 %copy-start.9 = (bf16[8192,128]{1,0:T(8,128)(2,1)S(1)}, bf16[8192,128]{1,0:T(8,128)(2,1)}, u32[]{:S(2)}) copy-start(bf16[8192,128]{1,0:T(8,128)(2,1)} %param.34) | copy-start | bytes 6291460
  402.2 16.2 %copy-start.10 = (bf16[8192,128]{1,0:T(8,128)(2,1)S(1)}, bf16[8192,128]{1,0:T(8,128)(2,1)}, u32[]{:S(2)}) copy-start(bf16[8192,128]{1,0:T(8,128)(2,1)} %param.35) | copy-start | bytes 6291460
  480.8 2.7 copy-start.1
Sparse Core Ops, SparseCore 0:
  30.0 80.6 all-reduce.1
  153.4 60.5 reduce-scatter.1
  216.0 32.1 all-gather.3
  256.6 115.3 all-gather.5
